TPU v7x, 32 devices: a whole 2x2x4 slice. The times are simulated.
32 devices in a mesh: fsdp: 2 (over core), ctx: 4 (over y, x), tp: 4 (over z).
Axes of the slice: x: 2, y: 2, z: 4, core: 2. Of those that a mesh axis runs over, the one named last changes fastest.
Arguments:
- layer_input: float32 [4, 1024, 512], P('fsdp', 'ctx'), may hold values from -6 to 6
- timesteps: int32 [4], P('fsdp'), may hold values from 0 to 999
- segment_ids: int32 [4, 1024], P('fsdp'), may hold values from 0 to 15, never falling along the last dimension, each value on 1 to 512 neighbouring positions
- time_table: float32 [1000, 512], replicated, may hold values from -3 to 3
- ln1_gain: float32 [512], replicated, may hold values from 0.5 to 1.5
- ln1_bias: float32 [512], replicated, may hold values from -1.5 to 1.5
- w_qkv: float32 [3, 512, 512], P(None, 'fsdp', 'tp'), may hold values from -0.25 to 0.25
- b_qv: float32 [2, 512], P(None, 'tp'), may hold values from -1.5 to 1.5
- w_out_t: float32 [512, 512], P('fsdp', 'tp'), may hold values from -1 to 1
- b_out: float32 [512], replicated, may hold values from -1.5 to 1.5
- ln2_gain: float32 [512], replicated, may hold values from 0.5 to 1.5
- ln2_bias: float32 [512], replicated, may hold values from -1.5 to 1.5
- w_up: float32 [512, 2048], P('fsdp', 'tp'), may hold values from -0.25 to 0.25
- b_up: float32 [2048], P('tp'), may hold values from -1.5 to 1.5
- w_down_t: float32 [512, 2048], P('fsdp', 'tp'), may hold values from -0.125 to 0.125
- b_down: float32 [512], replicated, may hold values from -1.5 to 1.5
- out_grad: float32 [4, 1024, 512], P('fsdp', 'ctx'), may hold values from -6 to 6
Outputs:
- output: float32 [4, 1024, 512], P('fsdp', 'ctx')
- grad_input: float32 [4, 1024, 512], P('fsdp', 'ctx')
- grad_table: float32 [1000, 512], replicated
- grad_ln1_gain: float32 [512], replicated
- grad_ln1_bias: float32 [512], replicated
- grad_w_qkv: float32 [3, 512, 512], P(None, 'fsdp', 'tp')
- grad_b_qv: float32 [2, 512], P(None, 'tp')
- grad_w_out_t: float32 [512, 512], P('fsdp', 'tp')
- grad_b_out: float32 [512], replicated
- grad_ln2_gain: float32 [512], replicated
- grad_ln2_bias: float32 [512], replicated
- grad_w_up: float32 [512, 2048], P('fsdp', 'tp')
- grad_b_up: float32 [2048], P('tp')
- grad_w_down_t: float32 [512, 2048], P('fsdp', 'tp')
- grad_b_down: float32 [512], replicated
Inputs may be any that keep to these rules, and one draw needn't show every extreme that they name: `segment_ids`: in each sequence the ids never fall; each document has 1 to 512 characters and one has exactly 512.
All inputs are finite; a program needn't handle non-finite values.
Results may differ from a plain program's by a relative error of at most 0.011.
Values may be sent and summed in bfloat16 or wider, within the bound.
No kernel may reach another device: no remote copies, remote signals or barrier semaphores. Data moves between devices by JAX's collectives and lax.ppermute only.
A program may use at most 64 MiB of HBM per device.

v0:
```python
import jax
import jax.numpy as jnp
from jax import lax
from jax.sharding import PartitionSpec as P

HEAD_DIM = 64
EPSILON = 1e-05
NEGATIVE = -1e30
PRECISE = lax.Precision.HIGHEST


def layer_norm(values, norm_gain, norm_bias):
    centre = values - jnp.mean(values, axis=-1, keepdims=True)
    spread = jnp.mean(centre * centre, axis=-1, keepdims=True)
    return centre * lax.rsqrt(spread + EPSILON) * norm_gain + norm_bias


def contract_last(left, right):
    return lax.dot_general(
        left, right, (((1,), (1,)), ((), ())), preferred_element_type=jnp.float32
    )


def contract_first(left, right):
    return lax.dot_general(
        left, right, (((0,), (0,)), ((), ())), preferred_element_type=jnp.float32
    )


def per_device(
    layer_input,
    timesteps,
    segment_ids,
    time_table,
    ln1_gain,
    ln1_bias,
    w_qkv,
    b_qv,
    w_out_t,
    b_out,
    ln2_gain,
    ln2_bias,
    w_up,
    b_up,
    w_down_t,
    b_down,
    out_grad,
):
    seq_count, span_len, model_width = layer_input.shape
    tok_rows = seq_count * span_len
    seq_len = segment_ids.shape[1]
    step_count = time_table.shape[0]
    ctx_index = lax.axis_index("ctx")
    masters = (
        w_qkv.astype(jnp.bfloat16),
        w_out_t.astype(jnp.bfloat16),
        w_up.astype(jnp.bfloat16),
        w_down_t.astype(jnp.bfloat16),
    )
    qkv_mat, out_mat, up_mat, down_mat = (
        lax.all_gather(masters[0], "fsdp", axis=1, tiled=True),
        lax.all_gather(masters[1], "fsdp", axis=0, tiled=True),
        lax.all_gather(masters[2], "fsdp", axis=0, tiled=True),
        lax.all_gather(masters[3], "fsdp", axis=0, tiled=True),
    )
    steps_hot = (timesteps[:, None] == jnp.arange(step_count, dtype=jnp.int32)[None, :]).astype(
        jnp.float32
    )
    embedded = jnp.dot(steps_hot, time_table, precision=PRECISE)
    stream = (layer_input + embedded[:, None, :]).reshape(tok_rows, model_width)
    normed, norm_one_pull = jax.vjp(layer_norm, stream, ln1_gain, ln1_bias)
    normed_low = normed.astype(jnp.bfloat16)
    projected = jnp.einsum("rd,kdc->krc", normed_low, qkv_mat, preferred_element_type=jnp.float32)
    local_cols = projected.shape[2]
    heads_here = local_cols // HEAD_DIM
    query = (projected[0] + b_qv[0]).astype(jnp.bfloat16)
    key_local = projected[1].astype(jnp.bfloat16).reshape(seq_count, span_len, local_cols)
    value_local = (
        (projected[2] + b_qv[1]).astype(jnp.bfloat16).reshape(seq_count, span_len, local_cols)
    )
    key_all, value_all = (
        lax.all_gather(key_local, "ctx", axis=1, tiled=True),
        lax.all_gather(value_local, "ctx", axis=1, tiled=True),
    )
    query_ids = lax.dynamic_slice_in_dim(segment_ids, ctx_index * span_len, span_len, 1)
    same_doc = (query_ids[:, :, None] == segment_ids[:, None, :])[:, None]
    query_heads = query.reshape(seq_count, span_len, heads_here, HEAD_DIM)
    key_heads = key_all.reshape(seq_count, seq_len, heads_here, HEAD_DIM)
    value_heads = value_all.reshape(seq_count, seq_len, heads_here, HEAD_DIM)
    scale = HEAD_DIM ** (-0.5)

    def score_block():
        raw_scores = jnp.einsum(
            "sqhd,skhd->shqk", query_heads, key_heads, preferred_element_type=jnp.float32
        )
        return jnp.where(same_doc, raw_scores * scale, NEGATIVE)

    scores = score_block()
    row_top = jnp.max(scores, axis=-1, keepdims=True)
    expd = jnp.exp(scores - row_top)
    row_total = jnp.sum(expd, axis=-1, keepdims=True)
    probs = expd / row_total
    log_total = row_top + jnp.log(row_total)
    mixed = jnp.einsum(
        "shqk,skhd->sqhd",
        probs.astype(jnp.bfloat16),
        value_heads,
        preferred_element_type=jnp.float32,
    )
    mixed = mixed.reshape(tok_rows, local_cols).astype(jnp.bfloat16)
    attn_terms = contract_last(mixed, out_mat)
    attn = lax.psum(attn_terms, "tp")
    resid = stream + attn + b_out
    normed_two, norm_two_pull = jax.vjp(layer_norm, resid, ln2_gain, ln2_bias)
    normed_two_low = normed_two.astype(jnp.bfloat16)
    pre_act = jnp.dot(normed_two_low, up_mat, preferred_element_type=jnp.float32) + b_up
    activ, gelu_pull = jax.vjp(jax.nn.gelu, pre_act)
    activ_low = activ.astype(jnp.bfloat16)
    ffn_terms = contract_last(activ_low, down_mat)
    ffn = lax.psum(ffn_terms.astype(jnp.bfloat16), "tp").astype(jnp.float32)
    output = (resid + ffn + b_down).reshape(seq_count, span_len, model_width)
    cotan = out_grad.reshape(tok_rows, model_width)
    cotan_low = cotan.astype(jnp.bfloat16)
    grad_down = contract_first(cotan_low, activ_low)
    grad_act = jnp.dot(cotan_low, down_mat, preferred_element_type=jnp.float32)
    (grad_pre,) = gelu_pull(grad_act)
    grad_pre_low = grad_pre.astype(jnp.bfloat16)
    grad_upmat = contract_first(normed_two_low, grad_pre_low)
    back_two = lax.psum(contract_last(grad_pre_low, up_mat), "tp")
    resid_back, grad_gain_two, grad_bias_two = norm_two_pull(back_two)
    grad_resid = cotan + resid_back
    grad_resid_low = grad_resid.astype(jnp.bfloat16)
    grad_outmat = contract_first(grad_resid_low, mixed)
    grad_mixed = jnp.dot(grad_resid_low, out_mat, preferred_element_type=jnp.float32).astype(
        jnp.bfloat16
    )
    probs_again = jnp.exp(score_block() - log_total)
    mixed_heads = grad_mixed.reshape(seq_count, span_len, heads_here, HEAD_DIM)
    grad_probs = jnp.einsum(
        "sqhd,skhd->shqk", mixed_heads, value_heads, preferred_element_type=jnp.float32
    )
    inner = jnp.sum(probs_again * grad_probs, axis=-1, keepdims=True)
    grad_raw = (probs_again * (grad_probs - inner) * scale).astype(jnp.bfloat16)
    grad_query = jnp.einsum(
        "shqk,skhd->sqhd", grad_raw, key_heads, preferred_element_type=jnp.float32
    ).reshape(tok_rows, local_cols)
    grad_key_all = jnp.einsum(
        "shqk,sqhd->skhd", grad_raw, query_heads, preferred_element_type=jnp.float32
    ).reshape(seq_count, seq_len, local_cols)
    grad_value_all = jnp.einsum(
        "shqk,sqhd->skhd",
        probs_again.astype(jnp.bfloat16),
        mixed_heads,
        preferred_element_type=jnp.float32,
    ).reshape(seq_count, seq_len, local_cols)
    grad_key, grad_value = (
        lax.psum_scatter(grad_key_all, "ctx", scatter_dimension=1, tiled=True),
        lax.psum_scatter(grad_value_all, "ctx", scatter_dimension=1, tiled=True),
    )
    grad_key = grad_key.reshape(tok_rows, local_cols)
    grad_value = grad_value.reshape(tok_rows, local_cols)
    grad_stack = jnp.stack(
        [
            grad_query.astype(jnp.bfloat16),
            grad_key.astype(jnp.bfloat16),
            grad_value.astype(jnp.bfloat16),
        ]
    )
    grad_qkvmat = jnp.einsum(
        "rd,krc->kdc", normed_low, grad_stack, preferred_element_type=jnp.float32
    )
    back_one = lax.psum(
        jnp.einsum("krc,kdc->rd", grad_stack, qkv_mat, preferred_element_type=jnp.float32), "tp"
    )
    stream_back, grad_gain_one, grad_bias_one = norm_one_pull(back_one)
    grad_input = grad_resid + stream_back
    per_sequence = jnp.sum(grad_input.reshape(seq_count, span_len, model_width), axis=1)
    qv_terms = jnp.stack([jnp.sum(grad_query, axis=0), jnp.sum(grad_value, axis=0)])
    small = lax.psum(
        (
            grad_gain_one,
            grad_bias_one,
            grad_gain_two,
            grad_bias_two,
            qv_terms,
            jnp.sum(grad_pre, axis=0),
            jnp.sum(grad_resid, axis=0),
            jnp.sum(cotan, axis=0),
        ),
        ("fsdp", "ctx"),
    )
    (
        gain_one_sum,
        bias_one_sum,
        gain_two_sum,
        bias_two_sum,
        qv_sum,
        up_bias_sum,
        out_bias_sum,
        down_bias_sum,
    ) = small
    table_terms = jnp.dot(steps_hot.T, per_sequence, precision=PRECISE)
    table_sum = lax.psum(table_terms, ("fsdp", "ctx"))
    weight_terms = (grad_qkvmat, grad_outmat, grad_upmat, grad_down)
    summed = lax.psum((weight_terms[0], weight_terms[1], weight_terms[2], weight_terms[3]), "ctx")
    owned = (
        lax.psum_scatter(summed[0], "fsdp", scatter_dimension=1, tiled=True),
        lax.psum_scatter(summed[1], "fsdp", scatter_dimension=0, tiled=True),
        lax.psum_scatter(summed[2], "fsdp", scatter_dimension=0, tiled=True),
        lax.psum_scatter(summed[3], "fsdp", scatter_dimension=0, tiled=True),
    )
    qkv_owned, out_owned, up_owned, down_owned = owned
    return (
        output,
        grad_input.reshape(seq_count, span_len, model_width),
        table_sum,
        gain_one_sum,
        bias_one_sum,
        qkv_owned,
        qv_sum,
        out_owned,
        out_bias_sum,
        gain_two_sum,
        bias_two_sum,
        up_owned,
        up_bias_sum,
        down_owned,
        down_bias_sum,
    )


def solution(mesh):
    placed = (
        P("fsdp", "ctx", None),
        P("fsdp"),
        P("fsdp", None),
        P(),
        P(),
        P(),
        P(None, "fsdp", "tp"),
        P(None, "tp"),
        P("fsdp", "tp"),
        P(),
        P(),
        P(),
        P("fsdp", "tp"),
        P("tp"),
        P("fsdp", "tp"),
        P(),
        P("fsdp", "ctx", None),
    )
    return jax.shard_map(
        per_device,
        mesh=mesh,
        in_specs=placed,
        out_specs=(
            P("fsdp", "ctx", None),
            P("fsdp", "ctx", None),
            P(),
            P(),
            P(),
            P(None, "fsdp", "tp"),
            P(None, "tp"),
            P("fsdp", "tp"),
            P(),
            P(),
            P(),
            P("fsdp", "tp"),
            P("tp"),
            P("fsdp", "tp"),
            P(),
        ),
        check_vma=False,
    )
```

profile of v0, /device:TPU:0, one launch (start us, length us, event | category | flops | bytes accessed | tf_op | source)
XLA Modules:
  0.0 526.8 jit_solution(3402038133135190457)
XLA Ops:
  8.4 2.2 all_gather.18
  17.8 2.0 all_gather.21
  21.0 2.1 reshape.228
  23.0 1.9 copy.60
  25.0 13.5 %all_gather.20 = bf16[2,1024,128]{2,1,0:T(8,128)(2,1)} all-gather(bf16[2,256,128]{2,1,0:T(8,128)(2,1)} %bitcast.102), channel_id=1, replica_groups=mesh['fsdp'=2,'ctx'=4,'tp'=4] {'ctx'}, dimensions={1}, use_global_device_ids=true | all-gather | bytes 655360 | tf_op jit(solution)/shard_map/all_gather | solution.py:82
  38.5 2.0 copy.61
  41.5 9.8 %all_gather.19 = bf16[2,1024,128]{2,1,0:T(8,128)(2,1)} all-gather(bf16[2,256,128]{2,1,0:T(8,128)(2,1)S(1)} %add_convert_fusion.3), channel_id=1, replica_groups=mesh['fsdp'=2,'ctx'=4,'tp'=4] {'ctx'}, dimensions={1}, use_global_device_ids=true | all-gather | bytes 655360 | tf_op jit(solution)/shard_map/all_gather | solution.py:83
  51.3 2.0 copy.58
  53.4 2.5 fusion.67
  62.4 2.3 all_gather.22
  64.7 2.3 all_gather.23
  70.8 41.6 %all-reduce.9.cloned.1.call-done = f32[512,512]{1,0:T(8,128)} async-done(((f32[512,512]{1,0:T(8,128)}), f32[512,512]{1,0:T(8,128)}) %all-reduce.9.cloned.1.call-update) | async-done | bytes 1048592 | tf_op jit(solution)/shard_map/psum | solution.py:112
  114.3 2.7 fusion.55
  119.3 2.7 convolution_convert_fusion
  122.3 48.4 %all-reduce.13.cloned.1.call-done = f32[512,512]{1,0:T(8,128)} async-done(((f32[512,512]{1,0:T(8,128)}), f32[512,512]{1,0:T(8,128)}) %all-reduce.13.cloned.1.call-update) | async-done | bytes 1048592 | tf_op jit(solution)/shard_map/psum | solution.py:129
  170.6 2.0 multiply_reduce_fusion.1
  172.6 38.1 %all-reduce.11.cloned.1.call-done = bf16[512,512]{1,0:T(8,128)(2,1)} async-done(((bf16[512,512]{1,0:T(8,128)(2,1)}), bf16[512,512]{1,0:T(8,128)(2,1)}) %all-reduce.11.cloned.1.call-update) | async-done | bytes 524304 | tf_op jit(solution)/shard_map/psum | solution.py:120
  210.7 3.2 fusion.59
  216.1 1.7 reshape.230
  217.9 1.7 copy.64
  219.6 4.1 fusion.12
  223.7 3.8 fusion.72
  227.6 12.8 %fusion.7 = f32[2,2,64,1024]{3,2,1,0:T(8,128)} fusion(f32[2,2,256,1024]{3,2,1,0:T(8,128)} %fusion.72, f32[2,2,256,1024]{3,2,1,0:T(8,128)} %copy-done.1, f32[2,2,256]{2,1,0:T(2,128)S(1)} %log_add_fusion, f32[2,256,2,64]{1,3,2,0:T(8,128)} %copy.60, f32[2,64]{1,0:T(2,128)S(1)} %add.179), kind=kOutput, calls=%fused_computation.10 | convolution fusion | flops 141690880 | bytes 9703936 | tf_op jit(solution)/shard_map/shqk,sqhd->skhd/dot_general | solution.py:147
  240.5 2.3 fusion.36
  242.8 2.9 convolution_bitcast_fusion
  245.8 3.1 fusion.39
  248.9 12.1 %fusion.65 = (f32[2,64]{1,0:T(2,128)S(1)}, bf16[2,256,2,64]{1,3,2,0:T(8,128)(2,1)}) fusion(bf16[2,1024,2,64]{1,3,2,0:T(8,128)(2,1)} %bitcast.90, f32[2,2,256,1024]{3,2,1,0:T(8,128)} %fusion.72, f32[2,2,256,1024]{3,2,1,0:T(8,128)} %copy-done.1, f32[2,2,256]{2,1,0:T(2,128)S(1)} %log_add_fusion), kind=kOutput, calls=%fused_computation.104 | convolution fusion | flops 141690752 | bytes 9048576 | tf_op jit(solution)/shard_map/shqk,skhd->sqhd/dot_general | solution.py:144
  261.0 1.8 copy.76
  262.8 1.8 reshape.229
  264.6 1.7 fusion.66
  266.3 1.7 copy.68
  268.0 14.4 %reduce-scatter.7.cloned.1.call-done = f32[2,256,128]{1,2,0:T(8,128)} async-done(((f32[2,1024,128]{1,2,0:T(8,128)}), f32[2,256,128]{1,2,0:T(8,128)}) %reduce-scatter.7.cloned.1.call-update) | async-done | bytes 262160 | tf_op jit(solution)/shard_map/reduce_scatter | solution.py:157
  285.6 2.5 convolution_bitcast_fusion.2
  288.2 2.5 convolution_bitcast_fusion.1
  290.8 1.9 reduce-scatter.13.cloned.1.call-done
  292.7 12.1 %reduce-scatter.17.cloned.1.call-done = f32[256,512]{0,1:T(8,128)} async-done(((f32[512,512]{0,1:T(8,128)}), f32[256,512]{0,1:T(8,128)}) %reduce-scatter.17.cloned.1.call-update) | async-done | bytes 524304 | tf_op jit(solution)/shard_map/reduce_scatter | solution.py:210
  304.8 12.0 %reduce-scatter.15.cloned.1.call-done = f32[256,512]{1,0:T(8,128)} async-done(((f32[512,512]{1,0:T(8,128)}), f32[256,512]{1,0:T(8,128)}) %reduce-scatter.15.cloned.1.call-update) | async-done | bytes 524304 | tf_op jit(solution)/shard_map/reduce_scatter | solution.py:209
  316.7 12.3 %reduce-scatter.11.cloned.1.call-done = f32[3,256,128]{1,2,0:T(8,128)} async-done(((f32[3,512,128]{1,2,0:T(8,128)}), f32[3,256,128]{1,2,0:T(8,128)}) %reduce-scatter.11.cloned.1.call-update) | async-done | bytes 393232 | tf_op jit(solution)/shard_map/reduce_scatter | solution.py:207
  329.4 55.5 %all-reduce.15.cloned.1.call-done = f32[512,512]{1,0:T(8,128)} async-done(((f32[512,512]{1,0:T(8,128)}), f32[512,512]{1,0:T(8,128)}) %all-reduce.15.cloned.1.call-update) | async-done | bytes 1048592 | tf_op jit(solution)/shard_map/psum | solution.py:172
  384.9 1.8 multiply_reduce_fusion.2
  386.7 1.8 fusion.58
  388.7 2.4 fusion.43
  391.2 27.6 %all-reduce = (f32[512]{0:T(512)}, f32[512]{0:T(512)}, f32[2,128]{1,0:T(2,128)}, f32[512]{0:T(512)}, f32[512]{0:T(512)}, /*index=5*/f32[512]{0:T(512)}, f32[512]{0:T(512)}, f32[512]{0:T(512)}) all-reduce(f32[512]{0:T(512)S(1)} %get-tuple-element.62, ...), channel_id=1, replica_groups=mesh['fsdp'=2,'ctx'=4,'tp'=4] {'fsdp','ctx'}, use_global_device_ids=true, to_apply=%region_20.21 | all-reduce | flops 3840 | bytes 30720 | tf_op jit(solution)/shard_map/psum | solution.py:179
  418.9 31.2 %all-reduce.19.cloned.1.call-done = (f32[3,256,128]{1,2,0:T(8,128)}, f32[256,128]{1,0:T(8,128)}, f32[256,512]{1,0:T(8,128)}, f32[256,512]{0,1:T(8,128)}) async-done(((f32[3,256,128]{1,2,0:T(8,128)}, f32[256,128]{1,0:T(8,128)}, f32[256,512]{1,0:T(8,128)}, f32[256,512]{0,1:T(8,128)}), (f32[3,256,128]{1,2,0:T(8,128)}, f32[256,128]{1,0:T(8,128)}, f32[256,512]{1,0:T(8,128)}, ...) | async-done | bytes 1572880 | tf_op jit(solution)/shard_map/psum | solution.py:205
  450.1 1.9 copy.71
  452.1 2.0 copy.72
  454.1 61.3 %all-reduce.17.cloned.1.call-done = f32[1000,512]{1,0:T(8,128)} async-done(((f32[1000,512]{1,0:T(8,128)}), f32[1000,512]{1,0:T(8,128)}) %all-reduce.17.cloned.1.call-update) | async-done | bytes 2048016 | tf_op jit(solution)/shard_map/psum | solution.py:203
  515.4 3.1 copy.92
  (135 shorter events, 33.1 us)
Async XLA Ops:
  7.2 3.4 copy-start
  7.2 6.6 %copy-start.20 = (f32[512]{0:T(512)S(1)}, f32[512]{0:T(512)}, u32[]{:S(2)}) copy-start(f32[512]{0:T(512)} %param.21) | copy-start | bytes 6148
  7.2 6.6 %copy-start.22 = (f32[512]{0:T(512)S(1)}, f32[512]{0:T(512)}, u32[]{:S(2)}) copy-start(f32[512]{0:T(512)} %param.22) | copy-start | bytes 6148
  7.2 105.2 %all-reduce.9.cloned.1.call-start = ((), (), s32[]{:S(2)}) async-start(), calls=%async_computation.6 | async-start | bytes 2097152 | tf_op jit(solution)/shard_map/psum | solution.py:112
  12.0 4.7 copy-start.29
  12.0 7.8 %copy-start.21 = (s32[2,1024]{1,0:T(2,128)S(1)}, s32[2,1024]{1,0:T(2,128)}, u32[]{:S(2)}) copy-start(s32[2,1024]{1,0:T(2,128)} %param.19) | copy-start | bytes 24580
  14.0 0.8 copy-start.5
  53.4 3.6 copy-start.8
  55.8 2.2 copy-start.1
  56.9 1.9 copy-start.13
  58.2 0.7 copy-start.15
  60.1 52.3 %copy-start.23 = (f32[512]{0:T(512)S(1)}, f32[512]{0:T(512)}, u32[]{:S(2)}) copy-start(f32[512]{0:T(512)} %param.26) | copy-start | bytes 6148
  60.2 110.5 %all-reduce.13.cloned.1.call-start = ((), (), s32[]{:S(2)}) async-start(), calls=%async_computation.8 | async-start | bytes 2097152 | tf_op jit(solution)/shard_map/psum | solution.py:129
  64.7 49.5 %copy-start.19 = (f32[512]{0:T(512)S(1)}, f32[512]{0:T(512)}, u32[]{:S(2)}) copy-start(f32[512]{0:T(512)} %param.27) | copy-start | bytes 6148
  64.7 49.6 %copy-start.25 = (f32[512]{0:T(512)S(1)}, f32[512]{0:T(512)}, u32[]{:S(2)}) copy-start(f32[512]{0:T(512)} %param.28) | copy-start | bytes 6148
  64.7 49.6 %copy-start.30 = (f32[512]{0:T(512)S(1)}, f32[512]{0:T(512)}, u32[]{:S(2)}) copy-start(f32[512]{0:T(512)} %param.30) | copy-start | bytes 6148
  67.0 1.6 copy-start.11
  68.6 0.8 copy-start.10
  112.4 1.9 copy-start.12
  112.4 1.9 copy-start.16
  113.9 3.0 copy-start.2
  117.0 0.8 copy-start.9
  117.8 92.9 %copy-start.24 = (f32[512]{0:T(512)S(1)}, f32[512]{0:T(512)}, u32[]{:S(2)}) copy-start(f32[512]{0:T(512)} %param.32) | copy-start | bytes 6148
  119.3 91.4 %all-reduce.11.cloned.1.call-start = ((), (), s32[]{:S(2)}) async-start(), calls=%async_computation.7 | async-start | bytes 1048576 | tf_op jit(solution)/shard_map/psum | solution.py:120
  122.0 142.5 %reduce-scatter.9.cloned.1.call-start = ((), (), s32[]{:S(2)}) async-start(), calls=%async_computation.10 | async-start | bytes 1310720 | tf_op jit(solution)/shard_map/reduce_scatter | solution.py:158
  210.7 3.2 copy-start.6
  210.7 4.5 copy-start.14
  214.1 1.1 copy-start.3
  223.7 58.7 %reduce-scatter.7.cloned.1.call-start = ((), (), s32[]{:S(2)}) async-start(), calls=%async_computation.9 | async-start | bytes 1310720 | tf_op jit(solution)/shard_map/reduce_scatter | solution.py:157
  240.4 5.4 %copy-start.26 = (f32[512]{0:T(512)S(1)}, f32[512]{0:T(512)}, u32[]{:S(2)}) copy-start(f32[512]{0:T(512)} %param.28) | copy-start | bytes 6148
  240.4 52.3 %reduce-scatter.13.cloned.1.call-start = ((), (), s32[]{:S(2)}) async-start(), calls=%async_computation.14 | async-start | bytes 393216 | tf_op jit(solution)/shard_map/reduce_scatter | solution.py:208
  242.7 62.0 %reduce-scatter.17.cloned.1.call-start = ((), (), s32[]{:S(2)}) async-start(), calls=%async_computation.16 | async-start | bytes 1572864 | tf_op jit(solution)/shard_map/reduce_scatter | solution.py:210
  245.7 71.0 %reduce-scatter.15.cloned.1.call-start = ((), (), s32[]{:S(2)}) async-start(), calls=%async_computation.15 | async-start | bytes 1572864 | tf_op jit(solution)/shard_map/reduce_scatter | solution.py:209
  248.9 80.2 %reduce-scatter.11.cloned.1.call-start = ((), (), s32[]{:S(2)}) async-start(), calls=%async_computation.13 | async-start | bytes 1179648 | tf_op jit(solution)/shard_map/reduce_scatter | solution.py:207
  288.2 96.7 %all-reduce.15.cloned.1.call-start = ((), (), s32[]{:S(2)}) async-start(), calls=%async_computation.11 | async-start | bytes 2097152 | tf_op jit(solution)/shard_map/psum | solution.py:172
  290.7 159.4 %all-reduce.19.cloned.1.call-start = ((), (), s32[]{:S(2)}) async-start(), calls=%async_computation.17 | async-start | bytes 3145728 | tf_op jit(solution)/shard_map/psum | solution.py:205
  329.1 186.3 %all-reduce.17.cloned.1.call-start = ((), (), s32[]{:S(2)}) async-start(), calls=%async_computation.12 | async-start | bytes 4096000 | tf_op jit(solution)/shard_map/psum | solution.py:203
  384.9 3.6 copy-start.4
  386.6 2.1 copy-start.27
  388.4 2.8 copy-start.28
  388.6 129.9 %copy-start.7 = (f32[512,512]{1,0:T(8,128)}, f32[512,512]{1,0:T(8,128)S(1)}, u32[]{:S(2)}) copy-start(f32[512,512]{1,0:T(8,128)S(1)} %add_add_fusion.2) | copy-start | bytes 3145732
  450.1 68.4 %copy-start.18 = (f32[256,128]{1,0:T(8,128)S(1)}, f32[256,128]{1,0:T(8,128)}, u32[]{:S(2)}) copy-start(f32[256,128]{1,0:T(8,128)} %get-tuple-element.117) | copy-start | bytes 393220
  515.4 3.8 copy-start.17
Sparse Core Ops, SparseCore 0:
  60.3 52.0 all-reduce.8
  119.4 51.1 all-reduce.12
  173.0 37.6 all-reduce.10
  223.8 27.7 reduce-scatter.8
  254.6 27.7 reduce-scatter.6
  285.0 7.6 reduce-scatter.12
  295.0 9.6 reduce-scatter.16
  307.0 9.6 reduce-scatter.14
  319.7 9.3 reduce-scatter.10
  331.9 52.9 all-reduce.14
  388.6 61.4 all-reduce.18
  453.8 61.5 all-reduce.16
where the time goes:
time: 528 us; the launch traced here: 527 us
  waiting for transfers between devices  329 us (62%)
  matrix products  64.3 us (12%)
  blocking collectives  59.8 us (11%)
  local copies, waits for them, and re-layouts  33 us (6%)
  other arithmetic  25.2 us (5%)
  between operations  14.6 us (3%)
    psum x1, waiting for transfers between devices, per_device(): table_sum = lax.psum(table_terms, ('fsdp', 'ctx'))  61.3 us
    psum x1, waiting for transfers between devices, per_device(): lax.psum(jnp.einsum('krc,kdc->rd', grad_stack, qkv_mat, preferred_element...  55.5 us
    psum x1, waiting for transfers between devices, per_device(): back_two = lax.psum(contract_last(grad_pre_low, up_mat), 'tp')  48.4 us
    psum x1, waiting for transfers between devices, per_device(): attn = lax.psum(attn_terms, 'tp')  41.6 us
    psum x1, waiting for transfers between devices, per_device(): ffn = lax.psum(ffn_terms.astype(jnp.bfloat16), 'tp').astype(jnp.float32)  38.1 us
    psum x1, waiting for transfers between devices, per_device(): lax.psum((weight_terms[0], weight_terms[1], weight_terms[2], weight_terms...  31.2 us
    psum x1, blocking collectives, per_device(): lax.psum((grad_gain_one, grad_bias_one, grad_gain_two, grad_bias_two, qv_...  27.6 us
    reduce_scatter x1, waiting for transfers between devices, per_device(): lax.psum_scatter(grad_key_all, 'ctx', scatter_dimension=1, tiled=True)  14.4 us
  transfers between devices with their start and end apart: 12, of which 11 were waited for; matrix products, arithmetic and copies ran while one was open for 14% of the time, Pallas kernels for 0%

commit v1 on v0

--- a/solution.py
+++ b/solution.py
@@ -177,17 +177,20 @@
     per_sequence = jnp.sum(grad_input.reshape(seq_count, span_len, model_width), axis=1)
     qv_terms = jnp.stack([jnp.sum(grad_query, axis=0), jnp.sum(grad_value, axis=0)])
     small = lax.psum(
-        (
-            grad_gain_one,
-            grad_bias_one,
-            grad_gain_two,
-            grad_bias_two,
-            qv_terms,
-            jnp.sum(grad_pre, axis=0),
-            jnp.sum(grad_resid, axis=0),
-            jnp.sum(cotan, axis=0),
+        lax.psum(
+            (
+                grad_gain_one,
+                grad_bias_one,
+                grad_gain_two,
+                grad_bias_two,
+                qv_terms,
+                jnp.sum(grad_pre, axis=0),
+                jnp.sum(grad_resid, axis=0),
+                jnp.sum(cotan, axis=0),
+            ),
+            "fsdp",
         ),
-        ("fsdp", "ctx"),
+        "ctx",
     )
     (
         gain_one_sum,

time: 528 us -> 528 us (level)
  blocking collectives: 59.8 us -> 52.3 us
  waiting for transfers between devices: 329 us -> 336 us
    psum x1, blocking collectives: 27.6 us -> 3.37 us  [per_device(): lax.psum((grad_gain_one, grad_bias_one, grad_gain_two, grad_bias_two, qv_...]
    psum x0 -> x1, blocking collectives: none -> 16.8 us  [per_device(): lax.psum(lax.psum((grad_gain_one, grad_bias_one, grad_gain_two, grad_bias...]
    psum x1, waiting for transfers between devices: 31.2 us -> 38.5 us  [per_device(): lax.psum((weight_terms[0], weight_terms[1], weight_terms[2], weight_terms...]
where the time goes in v1:
time: 528 us; the launch traced here: 527 us
  waiting for transfers between devices  336 us (64%)
  matrix products  64.3 us (12%)
  blocking collectives  52.3 us (10%)
  local copies, waits for them, and re-layouts  33 us (6%)
  other arithmetic  25.2 us (5%)
  between operations  14.6 us (3%)
    psum x1, waiting for transfers between devices, per_device(): table_sum = lax.psum(table_terms, ('fsdp', 'ctx'))  61.3 us
    psum x1, waiting for transfers between devices, per_device(): lax.psum(jnp.einsum('krc,kdc->rd', grad_stack, qkv_mat, preferred_element...  55.5 us
    psum x1, waiting for transfers between devices, per_device(): back_two = lax.psum(contract_last(grad_pre_low, up_mat), 'tp')  48.4 us
    psum x1, waiting for transfers between devices, per_device(): attn = lax.psum(attn_terms, 'tp')  41.6 us
    psum x1, waiting for transfers between devices, per_device(): lax.psum((weight_terms[0], weight_terms[1], weight_terms[2], weight_terms...  38.5 us
    psum x1, waiting for transfers between devices, per_device(): ffn = lax.psum(ffn_terms.astype(jnp.bfloat16), 'tp').astype(jnp.float32)  38.1 us
    psum x1, blocking collectives, per_device(): lax.psum(lax.psum((grad_gain_one, grad_bias_one, grad_gain_two, grad_bias...  16.8 us
    reduce_scatter x1, waiting for transfers between devices, per_device(): lax.psum_scatter(grad_key_all, 'ctx', scatter_dimension=1, tiled=True)  14.4 us
  transfers between devices with their start and end apart: 12, of which 11 were waited for; matrix products, arithmetic and copies ran while one was open for 14% of the time, Pallas kernels for 0%

profile of v1, /device:TPU:0, one launch (start us, length us, event | category | flops | bytes accessed | tf_op | source)
XLA Modules:
  0.0 526.6 jit_solution(13752148472991624702)
XLA Ops:
  8.4 2.2 all_gather.18
  17.8 2.0 all_gather.21
  21.0 2.1 reshape.228
  23.0 1.9 copy.60
  25.0 13.5 %all_gather.20 = bf16[2,1024,128]{2,1,0:T(8,128)(2,1)} all-gather(bf16[2,256,128]{2,1,0:T(8,128)(2,1)} %bitcast.102), channel_id=1, replica_groups=mesh['fsdp'=2,'ctx'=4,'tp'=4] {'ctx'}, dimensions={1}, use_global_device_ids=true | all-gather | bytes 655360 | tf_op jit(solution)/shard_map/all_gather | solution.py:82
  38.5 2.0 copy.61
  41.5 9.8 %all_gather.19 = bf16[2,1024,128]{2,1,0:T(8,128)(2,1)} all-gather(bf16[2,256,128]{2,1,0:T(8,128)(2,1)S(1)} %add_convert_fusion.3), channel_id=1, replica_groups=mesh['fsdp'=2,'ctx'=4,'tp'=4] {'ctx'}, dimensions={1}, use_global_device_ids=true | all-gather | bytes 655360 | tf_op jit(solution)/shard_map/all_gather | solution.py:83
  51.3 2.0 copy.58
  53.4 2.5 fusion.67
  62.4 2.3 all_gather.22
  64.7 2.3 all_gather.23
  70.8 41.6 %all-reduce.10.cloned.1.call-done = f32[512,512]{1,0:T(8,128)} async-done(((f32[512,512]{1,0:T(8,128)}), f32[512,512]{1,0:T(8,128)}) %all-reduce.10.cloned.1.call-update) | async-done | bytes 1048592 | tf_op jit(solution)/shard_map/psum | solution.py:112
  114.3 2.7 fusion.55
  119.3 2.7 convolution_convert_fusion
  122.3 48.4 %all-reduce.14.cloned.1.call-done = f32[512,512]{1,0:T(8,128)} async-done(((f32[512,512]{1,0:T(8,128)}), f32[512,512]{1,0:T(8,128)}) %all-reduce.14.cloned.1.call-update) | async-done | bytes 1048592 | tf_op jit(solution)/shard_map/psum | solution.py:129
  170.6 2.0 multiply_reduce_fusion.1
  172.6 38.1 %all-reduce.12.cloned.1.call-done = bf16[512,512]{1,0:T(8,128)(2,1)} async-done(((bf16[512,512]{1,0:T(8,128)(2,1)}), bf16[512,512]{1,0:T(8,128)(2,1)}) %all-reduce.12.cloned.1.call-update) | async-done | bytes 524304 | tf_op jit(solution)/shard_map/psum | solution.py:120
  210.7 3.2 fusion.59
  216.1 1.7 reshape.230
  217.9 1.7 copy.64
  219.6 4.1 fusion.12
  223.7 3.8 fusion.72
  227.6 12.8 %fusion.7 = f32[2,2,64,1024]{3,2,1,0:T(8,128)} fusion(f32[2,2,256,1024]{3,2,1,0:T(8,128)} %fusion.72, f32[2,2,256,1024]{3,2,1,0:T(8,128)} %copy-done.1, f32[2,2,256]{2,1,0:T(2,128)S(1)} %log_add_fusion, f32[2,256,2,64]{1,3,2,0:T(8,128)} %copy.60, f32[2,64]{1,0:T(2,128)S(1)} %add.195), kind=kOutput, calls=%fused_computation.10 | convolution fusion | flops 141690880 | bytes 9703936 | tf_op jit(solution)/shard_map/shqk,sqhd->skhd/dot_general | solution.py:147
  240.5 2.3 fusion.36
  242.8 2.9 convolution_bitcast_fusion
  245.8 3.1 fusion.39
  248.9 12.1 %fusion.65 = (f32[2,64]{1,0:T(2,128)S(1)}, bf16[2,256,2,64]{1,3,2,0:T(8,128)(2,1)}) fusion(bf16[2,1024,2,64]{1,3,2,0:T(8,128)(2,1)} %bitcast.90, f32[2,2,256,1024]{3,2,1,0:T(8,128)} %fusion.72, f32[2,2,256,1024]{3,2,1,0:T(8,128)} %copy-done.1, f32[2,2,256]{2,1,0:T(2,128)S(1)} %log_add_fusion), kind=kOutput, calls=%fused_computation.104 | convolution fusion | flops 141690752 | bytes 9048576 | tf_op jit(solution)/shard_map/shqk,skhd->sqhd/dot_general | solution.py:144
  261.0 1.8 copy.76
  262.8 1.8 reshape.229
  264.6 1.7 fusion.66
  268.0 14.4 %reduce-scatter.7.cloned.1.call-done = f32[2,256,128]{1,2,0:T(8,128)} async-done(((f32[2,1024,128]{1,2,0:T(8,128)}), f32[2,256,128]{1,2,0:T(8,128)}) %reduce-scatter.7.cloned.1.call-update) | async-done | bytes 262160 | tf_op jit(solution)/shard_map/reduce_scatter | solution.py:157
  285.6 2.5 convolution_bitcast_fusion.2
  288.2 2.5 convolution_bitcast_fusion.1
  290.8 1.9 reduce-scatter.13.cloned.1.call-done
  292.7 12.1 %reduce-scatter.17.cloned.1.call-done = f32[256,512]{0,1:T(8,128)} async-done(((f32[512,512]{0,1:T(8,128)}), f32[256,512]{0,1:T(8,128)}) %reduce-scatter.17.cloned.1.call-update) | async-done | bytes 524304 | tf_op jit(solution)/shard_map/reduce_scatter | solution.py:213
  304.8 12.0 %reduce-scatter.15.cloned.1.call-done = f32[256,512]{1,0:T(8,128)} async-done(((f32[512,512]{1,0:T(8,128)}), f32[256,512]{1,0:T(8,128)}) %reduce-scatter.15.cloned.1.call-update) | async-done | bytes 524304 | tf_op jit(solution)/shard_map/reduce_scatter | solution.py:212
  316.7 12.3 %reduce-scatter.11.cloned.1.call-done = f32[3,256,128]{1,2,0:T(8,128)} async-done(((f32[3,512,128]{1,2,0:T(8,128)}), f32[3,256,128]{1,2,0:T(8,128)}) %reduce-scatter.11.cloned.1.call-update) | async-done | bytes 393232 | tf_op jit(solution)/shard_map/reduce_scatter | solution.py:210
  329.4 55.5 %all-reduce.16.cloned.1.call-done = f32[512,512]{1,0:T(8,128)} async-done(((f32[512,512]{1,0:T(8,128)}), f32[512,512]{1,0:T(8,128)}) %all-reduce.16.cloned.1.call-update) | async-done | bytes 1048592 | tf_op jit(solution)/shard_map/psum | solution.py:172
  384.9 1.8 multiply_reduce_fusion.2
  386.7 1.8 fusion.58
  388.7 2.4 fusion.43
  391.2 3.4 all-reduce.2
  394.6 16.8 %all-reduce = (f32[512]{0:T(512)}, f32[512]{0:T(512)}, f32[2,128]{1,0:T(2,128)}, f32[512]{0:T(512)}, f32[512]{0:T(512)}, /*index=5*/f32[512]{0:T(512)}, f32[512]{0:T(512)}, f32[512]{0:T(512)}) all-reduce(f32[512]{0:T(512)S(1)} %get-tuple-element.78, f32[512]{0:T(512)S(1)} %get-tuple-element.79, ...), channel_id=1, replica_groups=mesh['fsdp'=2,'ctx'=4,'tp'=4] {'ctx'}, use_global_device_ids=true, to_apply=%region_21.22 | all-reduce | flops 3840 | bytes 30720 | tf_op jit(solution)/shard_map/psum | solution.py:179
  411.4 38.5 %all-reduce.20.cloned.1.call-done = (f32[3,256,128]{1,2,0:T(8,128)}, f32[256,128]{1,0:T(8,128)}, f32[256,512]{1,0:T(8,128)}, f32[256,512]{0,1:T(8,128)}) async-done(((f32[3,256,128]{1,2,0:T(8,128)}, f32[256,128]{1,0:T(8,128)}, f32[256,512]{1,0:T(8,128)}, f32[256,512]{0,1:T(8,128)}), (f32[3,256,128]{1,2,0:T(8,128)}, f32[256,128]{1,0:T(8,128)}, f32[256,512]{1,0:T(8,128)}, ...) | async-done | bytes 1572880 | tf_op jit(solution)/shard_map/psum | solution.py:208
  449.9 1.9 copy.71
  451.9 2.0 copy.72
  453.9 61.3 %all-reduce.18.cloned.1.call-done = f32[1000,512]{1,0:T(8,128)} async-done(((f32[1000,512]{1,0:T(8,128)}), f32[1000,512]{1,0:T(8,128)}) %all-reduce.18.cloned.1.call-update) | async-done | bytes 2048016 | tf_op jit(solution)/shard_map/psum | solution.py:206
  515.2 3.1 copy.92
  (136 shorter events, 34.8 us)
Async XLA Ops:
  7.2 3.4 copy-start
  7.2 6.6 %copy-start.20 = (f32[512]{0:T(512)S(1)}, f32[512]{0:T(512)}, u32[]{:S(2)}) copy-start(f32[512]{0:T(512)} %param.21) | copy-start | bytes 6148
  7.2 6.6 %copy-start.22 = (f32[512]{0:T(512)S(1)}, f32[512]{0:T(512)}, u32[]{:S(2)}) copy-start(f32[512]{0:T(512)} %param.22) | copy-start | bytes 6148
  7.2 105.2 %all-reduce.10.cloned.1.call-start = ((), (), s32[]{:S(2)}) async-start(), calls=%async_computation.6 | async-start | bytes 2097152 | tf_op jit(solution)/shard_map/psum | solution.py:112
  12.0 4.7 copy-start.29
  12.0 7.8 %copy-start.21 = (s32[2,1024]{1,0:T(2,128)S(1)}, s32[2,1024]{1,0:T(2,128)}, u32[]{:S(2)}) copy-start(s32[2,1024]{1,0:T(2,128)} %param.19) | copy-start | bytes 24580
  14.0 0.8 copy-start.5
  53.4 3.6 copy-start.8
  55.8 2.2 copy-start.1
  56.9 1.9 copy-start.13
  58.2 0.7 copy-start.15
  60.1 52.3 %copy-start.23 = (f32[512]{0:T(512)S(1)}, f32[512]{0:T(512)}, u32[]{:S(2)}) copy-start(f32[512]{0:T(512)} %param.26) | copy-start | bytes 6148
  60.2 110.5 %all-reduce.14.cloned.1.call-start = ((), (), s32[]{:S(2)}) async-start(), calls=%async_computation.8 | async-start | bytes 2097152 | tf_op jit(solution)/shard_map/psum | solution.py:129
  64.7 49.5 %copy-start.19 = (f32[512]{0:T(512)S(1)}, f32[512]{0:T(512)}, u32[]{:S(2)}) copy-start(f32[512]{0:T(512)} %param.27) | copy-start | bytes 6148
  64.7 49.6 %copy-start.25 = (f32[512]{0:T(512)S(1)}, f32[512]{0:T(512)}, u32[]{:S(2)}) copy-start(f32[512]{0:T(512)} %param.28) | copy-start | bytes 6148
  64.7 49.6 %copy-start.30 = (f32[512]{0:T(512)S(1)}, f32[512]{0:T(512)}, u32[]{:S(2)}) copy-start(f32[512]{0:T(512)} %param.30) | copy-start | bytes 6148
  67.0 1.6 copy-start.11
  68.6 0.8 copy-start.10
  112.4 1.9 copy-start.12
  112.4 1.9 copy-start.16
  113.9 3.0 copy-start.2
  117.0 0.8 copy-start.9
  117.8 92.9 %copy-start.24 = (f32[512]{0:T(512)S(1)}, f32[512]{0:T(512)}, u32[]{:S(2)}) copy-start(f32[512]{0:T(512)} %param.32) | copy-start | bytes 6148
  119.3 91.4 %all-reduce.12.cloned.1.call-start = ((), (), s32[]{:S(2)}) async-start(), calls=%async_computation.7 | async-start | bytes 1048576 | tf_op jit(solution)/shard_map/psum | solution.py:120
  122.0 142.5 %reduce-scatter.9.cloned.1.call-start = ((), (), s32[]{:S(2)}) async-start(), calls=%async_computation.10 | async-start | bytes 1310720 | tf_op jit(solution)/shard_map/reduce_scatter | solution.py:158
  210.7 3.2 copy-start.6
  210.7 4.5 copy-start.14
  214.1 1.1 copy-start.3
  223.7 58.7 %reduce-scatter.7.cloned.1.call-start = ((), (), s32[]{:S(2)}) async-start(), calls=%async_computation.9 | async-start | bytes 1310720 | tf_op jit(solution)/shard_map/reduce_scatter | solution.py:157
  240.4 5.4 %copy-start.26 = (f32[512]{0:T(512)S(1)}, f32[512]{0:T(512)}, u32[]{:S(2)}) copy-start(f32[512]{0:T(512)} %param.28) | copy-start | bytes 6148
  240.4 52.3 %reduce-scatter.13.cloned.1.call-start = ((), (), s32[]{:S(2)}) async-start(), calls=%async_computation.14 | async-start | bytes 393216 | tf_op jit(solution)/shard_map/reduce_scatter | solution.py:211
  242.7 62.0 %reduce-scatter.17.cloned.1.call-start = ((), (), s32[]{:S(2)}) async-start(), calls=%async_computation.16 | async-start | bytes 1572864 | tf_op jit(solution)/shard_map/reduce_scatter | solution.py:213
  245.7 71.0 %reduce-scatter.15.cloned.1.call-start = ((), (), s32[]{:S(2)}) async-start(), calls=%async_computation.15 | async-start | bytes 1572864 | tf_op jit(solution)/shard_map/reduce_scatter | solution.py:212
  248.9 80.2 %reduce-scatter.11.cloned.1.call-start = ((), (), s32[]{:S(2)}) async-start(), calls=%async_computation.13 | async-start | bytes 1179648 | tf_op jit(solution)/shard_map/reduce_scatter | solution.py:210
  288.2 96.7 %all-reduce.16.cloned.1.call-start = ((), (), s32[]{:S(2)}) async-start(), calls=%async_computation.11 | async-start | bytes 2097152 | tf_op jit(solution)/shard_map/psum | solution.py:172
  290.7 159.2 %all-reduce.20.cloned.1.call-start = ((), (), s32[]{:S(2)}) async-start(), calls=%async_computation.17 | async-start | bytes 3145728 | tf_op jit(solution)/shard_map/psum | solution.py:208
  329.1 186.1 %all-reduce.18.cloned.1.call-start = ((), (), s32[]{:S(2)}) async-start(), calls=%async_computation.12 | async-start | bytes 4096000 | tf_op jit(solution)/shard_map/psum | solution.py:206
  384.9 3.6 copy-start.4
  386.6 2.1 copy-start.27
  388.4 2.8 copy-start.28
  388.6 129.7 %copy-start.7 = (f32[512,512]{1,0:T(8,128)}, f32[512,512]{1,0:T(8,128)S(1)}, u32[]{:S(2)}) copy-start(f32[512,512]{1,0:T(8,128)S(1)} %add_add_fusion.2) | copy-start | bytes 3145732
  449.9 68.4 %copy-start.18 = (f32[256,128]{1,0:T(8,128)S(1)}, f32[256,128]{1,0:T(8,128)}, u32[]{:S(2)}) copy-start(f32[256,128]{1,0:T(8,128)} %get-tuple-element.125) | copy-start | bytes 393220
  515.2 3.8 copy-start.17
Sparse Core Ops, SparseCore 0:
  60.3 52.0 all-reduce.9
  119.4 51.1 all-reduce.13
  173.0 37.6 all-reduce.11
  223.8 27.7 reduce-scatter.8
  254.6 27.7 reduce-scatter.6
  285.0 7.6 reduce-scatter.12
  295.0 9.6 reduce-scatter.16
  307.0 9.6 reduce-scatter.14
  319.7 9.3 reduce-scatter.10
  331.9 52.9 all-reduce.15
  388.6 61.2 all-reduce.19
  453.6 61.5 all-reduce.17
